TPU v7x, 256 devices: a whole 4x4x8 slice. The times are simulated.
256 devices in a mesh: req: 32 (over x, y, core), tp: 8 (over z).
Axes of the slice: x: 4, y: 4, z: 8, core: 2. Of those that a mesh axis runs over, the one named last changes fastest.
Arguments:
- activations: bfloat16 [4096, 2560], P('req', 'tp'), may hold values from -12 to 12
- norm_gain: float32 [2560], replicated, may hold values from 0.1 to 1.9
- input_proj: bfloat16 [2560, 8, 480], P(None, 'tp'), may hold values from -0.125 to 0.125
- output_proj: bfloat16 [2560, 2560], P('tp'), may hold values from -0.125 to 0.125
- cache_pool: bfloat16 [3008, 8, 20480], P('req', 'tp'), may hold values from -103 to 103
- page_table: int32 [64, 32], replicated, may hold values from 0 to 93, as said below
- rebalance_plan: int32 [64, 32], replicated, may hold values from 0 to 31, as said below
- cached_lengths: int32 [64], replicated, may hold values from 1 to 4096, as said below
- token_positions: int32 [64, 64], replicated, may hold values from 1 to 4159, as said below
Outputs:
- attention_out: float32 [4096, 2560], P('req', 'tp')
Inputs may be any that keep to these rules, and one draw needn't show every extreme that they name: token_positions[r, t] = cached_lengths[r] + t. `cached_lengths`: cached tokens of request r before its new ones; in every draw all requests of some group have 4096. rebalance_plan[r, j] is the request's own group for j < 16 and another group for later pages; page 16 of the first request of group q lies in group (q + 16) % 32; at most 2 of the pages j >= 16 of one group's requests lie in any one other group, and some group receives 2 from one other group in every draw. `page_table`: slot of page j of request r in the pool of group rebalance_plan[r, j]; no two entries of the table name the same group and slot.
All inputs are finite; a program needn't handle non-finite values.
Results may differ from a plain program's by a relative error of at most 0.0095.
The roundings to bfloat16 on the way count: a program that leaves them out, or rounds other values in their place, can miss the bound.
Values may be sent and summed in bfloat16 or wider, within the bound.
A program may use at most 128 MiB of HBM per device.

v0:
```python
import jax
import jax.numpy as jnp
from jax import lax
from jax.sharding import PartitionSpec as P

HD = 80
WINDOW = 4096
PAGE = 128
KEEP = 16
NEW = 64
TAIL = 16
EPSILON = 1e-05
THETA = 10000.0
MASKED = -1e30


def rotate(values, places):
    half_dim = values.shape[-1] // 2
    frequency = THETA ** (-(jnp.arange(half_dim, dtype=jnp.float32) * 2.0 / values.shape[-1]))
    angles = places.astype(jnp.float32)[..., None] * frequency
    cosine = jnp.cos(angles)
    sine_part = jnp.sin(angles)
    front_half = values[..., :half_dim]
    back_half = values[..., half_dim:]
    return jnp.concatenate(
        [front_half * cosine - back_half * sine_part, back_half * cosine + front_half * sine_part],
        axis=-1,
    )


def page_valid(places, lengths_here, page_ids):
    key_pos = page_ids[:, :, None] * PAGE + jnp.arange(PAGE, dtype=jnp.int32)[None, None, :]
    inside = key_pos < lengths_here[:, None, None]
    in_window = places[:, None, :, None] - key_pos[:, :, None, :] < WINDOW
    return inside[:, :, None, :] & in_window


def page_stats(queries, pages, valid):
    head_dim = queries.shape[-1]
    unpacked = pages.reshape(pages.shape[:3] + (-1, 2, head_dim))
    cache_keys = unpacked[..., 0, :]
    cache_values = unpacked[..., 1, :]
    scores = jnp.einsum(
        "rtkgd,rjkpd->rjkgtp", queries, cache_keys, preferred_element_type=jnp.float32
    ) * head_dim ** (-0.5)
    valid_mask = valid[:, :, None, None]
    block_peaks = jnp.max(jnp.where(valid_mask, scores, MASKED), axis=-1)
    probabilities = jnp.where(valid_mask, jnp.exp(scores - block_peaks[..., None]), 0.0).astype(
        jnp.bfloat16
    )
    totals = jnp.sum(probabilities, axis=-1, dtype=jnp.float32)
    value_sums = jnp.einsum(
        "rjkgtp,rjkpd->rjkgtd", probabilities, cache_values, preferred_element_type=jnp.float32
    )
    return (block_peaks, totals, value_sums)


def new_stats(queries, new_keys, new_values):
    head_dim = queries.shape[-1]
    count = queries.shape[1]
    scores = jnp.einsum(
        "rtkgd,rukd->rkgtu", queries, new_keys, preferred_element_type=jnp.float32
    ) * head_dim ** (-0.5)
    causal = jnp.arange(count)[:, None] >= jnp.arange(count)[None, :]
    block_peaks = jnp.max(jnp.where(causal, scores, MASKED), axis=-1)
    probabilities = jnp.where(causal, jnp.exp(scores - block_peaks[..., None]), 0.0).astype(
        jnp.bfloat16
    )
    totals = jnp.sum(probabilities, axis=-1, dtype=jnp.float32)
    value_sums = jnp.einsum(
        "rkgtu,rukd->rkgtd", probabilities, new_values, preferred_element_type=jnp.float32
    )
    return (block_peaks, totals, value_sums)


def fold_blocks(block_peaks, totals, value_sums):
    top_peak = jnp.max(block_peaks, axis=1)
    weights = jnp.exp(block_peaks - top_peak[:, None])
    return (
        top_peak,
        jnp.sum(weights * totals, axis=1),
        jnp.sum(weights[..., None] * value_sums, axis=1),
    )


def join_pair(first_stats, second_stats):
    top_peak = jnp.maximum(first_stats[0], second_stats[0])
    weight_one = jnp.exp(first_stats[0] - top_peak)
    weight_two = jnp.exp(second_stats[0] - top_peak)
    totals = weight_one * first_stats[1] + weight_two * second_stats[1]
    value_sums = weight_one[..., None] * first_stats[2] + weight_two[..., None] * second_stats[2]
    return (top_peak, totals, value_sums)


def local(
    activations,
    norm_gain,
    input_proj,
    output_proj,
    cache_pool,
    page_table,
    rebalance_plan,
    cached_lengths,
    token_positions,
):
    group_index = lax.axis_index("req")
    group_count = lax.axis_size("req")
    tok_rows = activations.shape[0]
    req_here = tok_rows // NEW
    kv_local = input_proj.shape[1]
    model_width = input_proj.shape[0]
    group_size = input_proj.shape[2] // HD - 2
    gathered = lax.all_gather(activations, "tp", axis=1, tiled=True)
    widened = gathered.astype(jnp.float32)
    mean_square = jnp.mean(widened * widened, axis=1, keepdims=True)
    normed = (widened * lax.rsqrt(mean_square + EPSILON) * norm_gain).astype(jnp.bfloat16)
    projected = jnp.dot(
        normed, input_proj.reshape(model_width, -1), preferred_element_type=jnp.float32
    )
    projected = projected.reshape(tok_rows, kv_local, group_size + 2, HD)
    first_row = group_index * req_here
    my_places = lax.dynamic_slice_in_dim(token_positions, first_row, req_here, 0)
    my_lengths = lax.dynamic_slice_in_dim(cached_lengths, first_row, req_here, 0)
    my_table = lax.dynamic_slice_in_dim(page_table, first_row, req_here, 0)
    my_plan = lax.dynamic_slice_in_dim(rebalance_plan, first_row, req_here, 0)
    flat_places = my_places.reshape(tok_rows)
    queries = rotate(
        projected[:, :, :group_size],
        jnp.broadcast_to(flat_places[:, None, None], (tok_rows, kv_local, group_size)),
    )
    queries = queries.astype(jnp.bfloat16).reshape(req_here, NEW, kv_local, group_size, HD)
    new_keys = rotate(projected[:, :, group_size], flat_places[:, None])
    new_keys = new_keys.astype(jnp.bfloat16).reshape(req_here, NEW, kv_local, HD)
    new_values = (
        projected[:, :, group_size + 1].astype(jnp.bfloat16).reshape(req_here, NEW, kv_local, HD)
    )
    fresh_stats = new_stats(queries, new_keys, new_values)
    tail_len = TAIL
    entries = req_here * tail_len
    capacity = (entries + group_count - 2) // (group_count - 1)
    home_ids = jnp.broadcast_to(jnp.arange(KEEP, dtype=jnp.int32)[None, :], (req_here, KEEP))
    tail_ids = jnp.broadcast_to(
        KEEP + jnp.arange(tail_len, dtype=jnp.int32)[None, :], (req_here, tail_len)
    )
    home_pages = cache_pool[my_table[:, :KEEP]]
    tail_plan = rebalance_plan[:, KEEP:].reshape(group_count, entries)
    tail_table = page_table[:, KEEP:].reshape(group_count, entries)
    held_here = tail_plan == group_index
    held_rank = jnp.cumsum(held_here.astype(jnp.int32), axis=1) - 1
    picked = held_here[:, :, None] & (
        held_rank[:, :, None] == jnp.arange(capacity, dtype=jnp.int32)[None, None, :]
    )
    entry_ids = jnp.sum(
        jnp.where(picked, jnp.arange(entries, dtype=jnp.int32)[None, :, None], 0), axis=1
    )
    send_slots = jnp.take_along_axis(tail_table, entry_ids, axis=1)
    outgoing = cache_pool[send_slots]
    own_plan = my_plan[:, KEEP:].reshape(entries)
    at_group = own_plan[:, None] == jnp.arange(group_count, dtype=jnp.int32)[None, :]
    own_rank = jnp.sum(
        jnp.where(at_group, jnp.cumsum(at_group.astype(jnp.int32), axis=0) - 1, 0), axis=1
    )
    flat_index = own_plan * capacity + own_rank
    received = lax.all_to_all(outgoing, "req", split_axis=0, concat_axis=0, tiled=True)
    tail_pages = received.reshape(group_count * capacity, kv_local, -1)[flat_index].reshape(
        req_here, tail_len, kv_local, -1
    )
    dense_pages = jnp.concatenate([home_pages, tail_pages], axis=1)
    all_ids = jnp.concatenate([home_ids, tail_ids], axis=1)
    combined = fold_blocks(
        *page_stats(queries, dense_pages, page_valid(my_places, my_lengths, all_ids))
    )
    merged = join_pair(combined, fresh_stats)
    heads_out = merged[2] / merged[1][..., None]
    heads_out = jnp.transpose(heads_out, (0, 3, 1, 2, 4)).reshape(tok_rows, -1).astype(jnp.bfloat16)
    partial_value = jnp.dot(heads_out, output_proj, preferred_element_type=jnp.float32)
    return lax.psum_scatter(partial_value, "tp", scatter_dimension=1, tiled=True)


def solution(mesh):
    in_specs = (
        P("req", "tp"),
        P(),
        P(None, "tp", None),
        P("tp", None),
        P("req", "tp", None),
        P(),
        P(),
        P(),
        P(),
    )
    out_specs = P("req", "tp")
    return jax.shard_map(local, mesh=mesh, in_specs=in_specs, out_specs=out_specs, check_vma=False)
```

profile of v0, /device:TPU:4, one launch (start us, length us, event | category | flops | bytes accessed | tf_op | source)
XLA Modules:
  0.0 170.4 jit_solution(8499491559643690964)
XLA Ops:
  6.5 0.9 slice_compare_fusion
  7.6 0.7 slice.42
  9.0 0.8 gather_fusion.3
  10.2 8.6 %gather_fusion.1 = bf16[64,20480]{1,0:T(8,128)(2,1)} fusion(bf16[94,20480]{1,0:T(8,128)(2,1)} %bitcast.127, s32[1024]{0:T(1024)S(1)} %pad_clamp_fusion.1), kind=kCustom, calls=%fused_computation.1 | custom fusion | bytes 5243136 | tf_op jit(solution)/shard_map/gather | solution.py:157
  18.8 4.8 %reshape.491 = bf16[32,2,1,20480]{3,1,0,2:T(2,128)(2,1)} reshape(bf16[64,20480]{1,0:T(8,128)(2,1)} %gather_fusion.1) | data formatting | bytes 5242880 | tf_op jit(solution)/shard_map/gather | solution.py:157
  23.6 7.8 %all-to-all-start = ((bf16[32,2,1,20480]{3,1,2,0:T(2,128)(2,1)}), bf16[32,2,1,20480]{3,1,2,0:T(2,128)(2,1)}, u32[]{:S(2)}, u32[]{:S(2)}) async-start(bf16[32,2,1,20480]{3,1,2,0:T(2,128)(2,1)} %bitcast.129), calls=%async_computation | async-start | bytes 5242880 | tf_op jit(solution)/shard_map/all_to_all | solution.py:164
  31.8 1.2 fusion.61
  33.1 29.3 %all_gather.3 = bf16[128,2560]{0,1:T(8,128)(2,1)S(1)} all-gather(bf16[128,320]{0,1:T(8,128)(2,1)S(1)} %copy-done.3), channel_id=1, replica_groups=mesh['req'=32,'tp'=8] {'tp'}, dimensions={1}, use_global_device_ids=true | all-gather | bytes 737280 | tf_op jit(solution)/shard_map/all_gather | solution.py:113
  62.3 0.4 fusion.10
  62.7 0.9 convolution_bitcast_fusion
  65.4 6.2 %gather_fusion = bf16[32,20480]{1,0:T(8,128)(2,1)} fusion(bf16[94,20480]{1,0:T(8,128)(2,1)} %bitcast.128, s32[1024]{0:T(1024)S(1)} %pad_clamp_fusion.2), kind=kCustom, calls=%fused_computation | custom fusion | bytes 2621568 | tf_op jit(solution)/shard_map/gather | solution.py:145
  71.7 4.5 %concatenate.44 = bf16[2,16,1,128,2,80]{5,4,3,1,0,2:T(2,128)(2,1)} reshape(bf16[32,20480]{1,0:T(8,128)(2,1)} %gather_fusion) | data formatting | bytes 2621440 | tf_op jit(solution)/shard_map/concatenate | solution.py:168
  76.2 5.9 %copy.87 = bf16[2,16,1,128,2,80]{3,5,1,0,4,2:T(8,128)(2,1)} copy(bf16[2,16,1,128,2,80]{5,4,3,1,0,2:T(2,128)(2,1)} %concatenate.44) | data formatting | bytes 2621440 | tf_op jit(solution)/shard_map/concatenate | solution.py:168
  82.3 0.6 pad_clamp_fusion
  83.5 1.2 fusion.9
  84.7 4.4 %reshape.500 = bf16[64,20480]{1,0:T(8,128)(2,1)} reshape(bf16[32,2,1,20480]{3,1,2,0:T(2,128)(2,1)} %all-to-all-done) | data formatting | bytes 5242880 | tf_op jit(solution)/shard_map/reshape | solution.py:165
  89.1 5.8 %gather_fusion.2 = bf16[32,20480]{1,0:T(8,128)(2,1)} fusion(bf16[64,20480]{1,0:T(8,128)(2,1)} %reshape.500, s32[1024]{0:T(1024)} %pad_clamp_fusion), kind=kCustom, calls=%fused_computation.2 | custom fusion | bytes 2621568 | tf_op jit(solution)/shard_map/gather | solution.py:165
  94.9 4.5 %concatenate.45 = bf16[2,16,1,128,2,80]{5,4,3,1,0,2:T(2,128)(2,1)} reshape(bf16[32,20480]{1,0:T(8,128)(2,1)} %gather_fusion.2) | data formatting | bytes 2621440 | tf_op jit(solution)/shard_map/concatenate | solution.py:168
  99.5 5.9 %copy.88 = bf16[2,16,1,128,2,80]{3,5,1,0,4,2:T(8,128)(2,1)} copy(bf16[2,16,1,128,2,80]{5,4,3,1,0,2:T(2,128)(2,1)} %concatenate.45) | data formatting | bytes 2621440 | tf_op jit(solution)/shard_map/concatenate | solution.py:168
  105.4 4.0 %fusion.3 = (f32[2,32,4,64]{3,2,1,0:T(4,128)S(1)}, f32[2,32,128,64,4]{2,3,4,1,0:T(8,128)S(1)}) fusion(pred[2,32,64,128]{3,2,1,0:T(8,128)(4,1)S(1)} %fusion.9, bf16[2,64,4,40]{3,1,2,0:T(8,128)(2,1)S(1)} %copy.91, bf16[2,64,4,40]{3,1,2,0:T(8,128)(2,1)S(1)} %copy.90, bf16[2,16,1,128,2,80]{3,5,1,0,4,2:T(8,128)(2,1)} %copy.87, ...), kind=kOutput, calls=%fused_computation.11 | convolution fusion | flops 344604672 | bytes 11681792 | tf_op jit(solution)/shard_map/rtkgd,rjkpd->rjkgtp/dot_general | solution.py:43
  109.4 5.8 %convert_reduce_fusion = (f32[2,32,4,64]{3,2,1,0:T(4,128)S(1)}, f32[2,4,64]{2,1,0:T(4,128)S(1)}) fusion(f32[2,32,4,64]{3,2,1,0:T(4,128)S(1)} %get-tuple-element.18, f32[2,32,128,64,4]{2,3,4,1,0:T(8,128)S(1)} %get-tuple-element.19, pred[2,32,64,128]{3,2,1,0:T(8,128)(4,1)S(1)} %fusion.9), kind=kLoop, calls=%fused_computation.9 | loop fusion | flops 16760320 | bytes 9046016 | tf_op jit(solution)/shard_map/reduce_sum | solution.py:51
  115.4 5.1 %multiply_reduce_fusion = f32[2,4,64,80]{3,2,1,0:T(8,128)S(1)} fusion(f32[2,32,4,64]{3,2,1,0:T(4,128)S(1)} %get-tuple-element.11, bf16[2,16,1,128,2,80]{3,5,1,0,4,2:T(8,128)(2,1)S(1)} %copy-done.2, bf16[2,16,1,128,2,80]{3,5,1,0,4,2:T(8,128)(2,1)S(1)} %copy-done.1, f32[2,32,128,64,4]{2,3,4,1,0:T(8,128)S(1)} %get-tuple-element.19, ...), kind=kOutput, calls=%fused_computation.10 | convolution fusion | flops 347168768 | bytes 11829248 | tf_op jit(solution)/shard_map/rjkgtp,rjkpd->rjkgtd/dot_general | solution.py:52
  121.1 3.4 %fusion.62 = f32[128,2560]{0,1:T(8,128)} fusion(bf16[128,320]{1,0:T(8,128)(2,1)S(1)} %convert_element_type.92, bf16[320,2560]{1,0:T(8,128)(2,1)} %param.12), kind=kOutput, calls=%fused_computation.112 | convolution fusion | flops 209715200 | bytes 3031040 | tf_op jit(solution)/shard_map/dot_general | solution.py:176
  124.5 39.0 %reduce-scatter.2.cloned.1.call-done = f32[128,320]{0,1:T(8,128)} async-done(((f32[128,2560]{0,1:T(8,128)}), f32[128,320]{0,1:T(8,128)}) %reduce-scatter.2.cloned.1.call-update) | async-done | bytes 163856 | tf_op jit(solution)/shard_map/reduce_scatter | solution.py:177
  (78 shorter events, 4.9 us)
Async XLA Ops:
  6.5 56.2 %copy-start = (bf16[2560,1,480]{0,2,1:T(8,128)(2,1)S(1)}, bf16[2560,1,480]{0,2,1:T(8,128)(2,1)}, u32[]{:S(2)}) copy-start(bf16[2560,1,480]{0,2,1:T(8,128)(2,1)} %param.11) | copy-start | bytes 7372804
  23.6 7.9 %copy-start.4 = (s32[64,32]{0,1:T(8,128)S(1)}, s32[64,32]{0,1:T(8,128)}, u32[]{:S(2)}) copy-start(s32[64,32]{0,1:T(8,128)} %param.15) | copy-start | bytes 24580
  23.6 8.2 %copy-start.5 = (s32[64,32]{0,1:T(8,128)S(1)}, s32[64,32]{0,1:T(8,128)}, u32[]{:S(2)}) copy-start(s32[64,32]{0,1:T(8,128)} %param.14) | copy-start | bytes 24580
  23.6 9.5 %copy-start.3 = (bf16[128,320]{0,1:T(8,128)(2,1)S(1)}, bf16[128,320]{0,1:T(8,128)(2,1)}, u32[]{:S(2)}) copy-start(bf16[128,320]{0,1:T(8,128)(2,1)} %param.9) | copy-start | bytes 245764
  23.6 39.2 %copy-start.6 = (f32[2560]{0:T(1024)S(1)}, f32[2560]{0:T(1024)}, u32[]{:S(2)}) copy-start(f32[2560]{0:T(1024)} %param.10) | copy-start | bytes 30724
  23.6 61.1 %all-to-all-start = ((bf16[32,2,1,20480]{3,1,2,0:T(2,128)(2,1)}), bf16[32,2,1,20480]{3,1,2,0:T(2,128)(2,1)}, u32[]{:S(2)}, u32[]{:S(2)}) async-start(bf16[32,2,1,20480]{3,1,2,0:T(2,128)(2,1)} %bitcast.129), calls=%async_computation | async-start | bytes 5242880 | tf_op jit(solution)/shard_map/all_to_all | solution.py:164
  31.4 32.3 %copy-start.7 = (s32[64]{0:T(128)S(1)}, s32[64]{0:T(128)}, u32[]{:S(2)}) copy-start(s32[64]{0:T(128)} %param.16) | copy-start | bytes 772
  31.4 132.2 %reduce-scatter.2.cloned.1.call-start = ((), (), s32[]{:S(2)}) async-start(), calls=%async_computation.2 | async-start | bytes 1474560 | tf_op jit(solution)/shard_map/reduce_scatter | solution.py:177
  109.4 5.9 %copy-start.1 = (bf16[2,16,1,128,2,80]{3,5,1,0,4,2:T(8,128)(2,1)S(1)}, bf16[2,16,1,128,2,80]{3,5,1,0,4,2:T(8,128)(2,1)}, u32[]{:S(2)}) copy-start(bf16[2,16,1,128,2,80]{3,5,1,0,4,2:T(8,128)(2,1)} %copy.87) | copy-start | bytes 3932164
  109.4 5.9 %copy-start.2 = (bf16[2,16,1,128,2,80]{3,5,1,0,4,2:T(8,128)(2,1)S(1)}, bf16[2,16,1,128,2,80]{3,5,1,0,4,2:T(8,128)(2,1)}, u32[]{:S(2)}) copy-start(bf16[2,16,1,128,2,80]{3,5,1,0,4,2:T(8,128)(2,1)} %copy.88) | copy-start | bytes 3932164
Sparse Core Ops, SparseCore 0:
  124.6 38.8 reduce-scatter.1
where the time goes:
time: 171 us; the launch traced here: 170 us
  local copies, waits for them, and re-layouts  55 us (32%)
  waiting for transfers between devices  39 us (23%)
  blocking collectives  29.3 us (17%)
  matrix products  14.1 us (8%)
  between operations  13.7 us (8%)
  other arithmetic  11.5 us (7%)
  starting transfers between devices  7.83 us (5%)
    reduce_scatter x1, waiting for transfers between devices, local(): lax.psum_scatter(partial_value, 'tp', scatter_dimension=1, tiled=True)  39 us
    all_gather x1, blocking collectives, local(): gathered = lax.all_gather(activations, 'tp', axis=1, tiled=True)  29.3 us
    concatenate x4, local copies, waits for them, and re-layouts, local(): dense_pages = jnp.concatenate([home_pages, tail_pages], axis=1)  20.9 us
    gather x2, local copies, waits for them, and re-layouts, local(): outgoing = cache_pool[send_slots]  13.3 us
    all_to_all x1, starting transfers between devices, local(): lax.all_to_all(outgoing, 'req', split_axis=0, concat_axis=0, tiled=True)  7.79 us
    gather x1, local copies, waits for them, and re-layouts, local(): home_pages = cache_pool[my_table[:, :KEEP]]  6.23 us
    reduce_sum x1, other arithmetic, page_stats(): totals = jnp.sum(probabilities, axis=-1, dtype=jnp.float32)  5.84 us
    gather x1, local copies, waits for them, and re-layouts, local(): received.reshape(group_count * capacity, kv_local, -1)[flat_index]  5.8 us
  transfers between devices with their start and end apart: 2, of which 1 were waited for; matrix products, arithmetic and copies ran while one was open for 14% of the time, Pallas kernels for 0%

commit v1 on v0

--- a/solution.py
+++ b/solution.py
@@ -12,6 +12,27 @@
 EPSILON = 1e-05
 THETA = 10000.0
 MASKED = -1e30
+
+
+def ring_gather(x, axis, dim):
+    devices, position, rows = (lax.axis_size(axis), lax.axis_index(axis), x.shape[dim])
+    ahead = [(i, (i + 1) % devices) for i in range(devices)]
+    backward = [(i, (i - 1) % devices) for i in range(devices)]
+    out = jnp.zeros((*x.shape[:dim], devices * rows, *x.shape[dim + 1 :]), x.dtype)
+    out = lax.dynamic_update_slice_in_dim(out, x, position * rows, axis=dim)
+    from_left = from_right = x
+    middle = devices // 2
+    for hop in range(1, middle + 1):
+        from_left = lax.ppermute(from_left, axis, ahead)
+        out = lax.dynamic_update_slice_in_dim(
+            out, from_left, (position - hop) % devices * rows, axis=dim
+        )
+        if hop < devices - middle:
+            from_right = lax.ppermute(from_right, axis, backward)
+            out = lax.dynamic_update_slice_in_dim(
+                out, from_right, (position + hop) % devices * rows, axis=dim
+            )
+    return out
 
 
 def rotate(values, places):
@@ -110,7 +131,7 @@
     kv_local = input_proj.shape[1]
     model_width = input_proj.shape[0]
     group_size = input_proj.shape[2] // HD - 2
-    gathered = lax.all_gather(activations, "tp", axis=1, tiled=True)
+    gathered = ring_gather(activations, "tp", 1)
     widened = gathered.astype(jnp.float32)
     mean_square = jnp.mean(widened * widened, axis=1, keepdims=True)
     normed = (widened * lax.rsqrt(mean_square + EPSILON) * norm_gain).astype(jnp.bfloat16)

time: 171 us -> 171 us (level)
  blocking collectives: 29.3 us -> 0 us
  starting transfers between devices: 7.83 us -> 20.5 us
  local copies, waits for them, and re-layouts: 55 us -> 66.4 us
  waiting for transfers between devices: 39 us -> 42.9 us
    all_gather x1 -> x0, blocking collectives: 29.3 us -> none  [local(): gathered = lax.all_gather(activations, 'tp', axis=1, tiled=True)]
    ppermute x0 -> x7, starting transfers between devices: none -> 12.5 us  [the longest x3 12.4 us: ring_gather(): from_right = lax.ppermute(from_right, axis, backward)]
    dynamic_update_slice x0 -> x8, local copies, waits for them, and re-layouts: none -> 7.21 us  [the longest x4 3.46 us: ring_gather(): lax.dynamic_update_slice_in_dim(out, from_left, (position - hop) % device...]
    ppermute x0 -> x7, waiting for transfers between devices: none -> 4.45 us  [the longest x4 4.44 us: ring_gather(): from_left = lax.ppermute(from_left, axis, ahead)]
    ppermute x0 -> x7, local copies, waits for them, and re-layouts: none -> 3.49 us  [the longest x4 2.25 us: ring_gather(): from_left = lax.ppermute(from_left, axis, ahead)]
  transfers between devices with their start and end apart: 2 -> 9, of which waited for: 1 -> 3; matrix products, arithmetic and copies ran while one was open for 14% -> 31% of each run, Pallas kernels for 0% -> 0%
where the time goes in v1:
time: 171 us; the launch traced here: 170 us
  local copies, waits for them, and re-layouts  66.4 us (39%)
  waiting for transfers between devices  42.9 us (25%)
  starting transfers between devices  20.5 us (12%)
  matrix products  14 us (8%)
  between operations  13.9 us (8%)
  other arithmetic  11.9 us (7%)
    reduce_scatter x1, waiting for transfers between devices, local(): lax.psum_scatter(partial_value, 'tp', scatter_dimension=1, tiled=True)  38.4 us
    concatenate x4, local copies, waits for them, and re-layouts, local(): dense_pages = jnp.concatenate([home_pages, tail_pages], axis=1)  21 us
    gather x2, local copies, waits for them, and re-layouts, local(): outgoing = cache_pool[send_slots]  13.3 us
    ppermute x3, starting transfers between devices, ring_gather(): from_right = lax.ppermute(from_right, axis, backward)  12.4 us
    all_to_all x1, starting transfers between devices, local(): lax.all_to_all(outgoing, 'req', split_axis=0, concat_axis=0, tiled=True)  7.79 us
    gather x1, local copies, waits for them, and re-layouts, local(): home_pages = cache_pool[my_table[:, :KEEP]]  6.22 us
    reduce_sum x1, other arithmetic, page_stats(): totals = jnp.sum(probabilities, axis=-1, dtype=jnp.float32)  5.84 us
    gather x1, local copies, waits for them, and re-layouts, local(): received.reshape(group_count * capacity, kv_local, -1)[flat_index]  5.68 us
  transfers between devices with their start and end apart: 9, of which 3 were waited for; matrix products, arithmetic and copies ran while one was open for 31% of the time, Pallas kernels for 0%

profile of v1, /device:TPU:4, one launch (start us, length us, event | category | flops | bytes accessed | tf_op | source)
XLA Modules:
  0.0 169.6 jit_solution(5167745974441755544)
XLA Ops:
  6.5 5.9 %collective-permute-start.1 = (bf16[128,320]{0,1:T(8,128)(2,1)}, bf16[128,320]{0,1:T(8,128)(2,1)S(1)}, u32[]{:S(2)}, u32[]{:S(2)}) collective-permute-start(bf16[128,320]{0,1:T(8,128)(2,1)} %param.9), channel_id=1, source_target_pairs={{0,7},{1,0},{2,1},{3,2},{4,3},{5,4},{6,5},{7,6},{8,15},{9,8},{10,9... | collective-permute-start | bytes 245768 | tf_op jit(solution)/shard_map/ppermute | solution.py:31
  15.9 8.6 %gather_fusion.1 = bf16[64,20480]{1,0:T(8,128)(2,1)} fusion(bf16[94,20480]{1,0:T(8,128)(2,1)} %bitcast.127, s32[1024]{0:T(1024)S(1)} %pad_clamp_fusion.1), kind=kCustom, calls=%fused_computation.1 | custom fusion | bytes 5243136 | tf_op jit(solution)/shard_map/gather | solution.py:178
  24.5 4.8 %reshape.491 = bf16[32,2,1,20480]{3,1,0,2:T(2,128)(2,1)} reshape(bf16[64,20480]{1,0:T(8,128)(2,1)} %gather_fusion.1) | data formatting | bytes 5242880 | tf_op jit(solution)/shard_map/gather | solution.py:178
  29.3 7.8 %all-to-all-start = ((bf16[32,2,1,20480]{3,1,2,0:T(2,128)(2,1)}), bf16[32,2,1,20480]{3,1,2,0:T(2,128)(2,1)}, u32[]{:S(2)}, u32[]{:S(2)}) async-start(bf16[32,2,1,20480]{3,1,2,0:T(2,128)(2,1)} %bitcast.129), calls=%async_computation | async-start | bytes 5242880 | tf_op jit(solution)/shard_map/all_to_all | solution.py:185
  40.0 1.4 fusion.9
  41.4 6.2 %gather_fusion = bf16[32,20480]{1,0:T(8,128)(2,1)} fusion(bf16[94,20480]{1,0:T(8,128)(2,1)} %bitcast.128, s32[1024]{0:T(1024)S(1)} %pad_clamp_fusion.2), kind=kCustom, calls=%fused_computation | custom fusion | bytes 2621568 | tf_op jit(solution)/shard_map/gather | solution.py:166
  47.6 4.5 %concatenate.44 = bf16[2,16,1,128,2,80]{5,4,3,1,0,2:T(2,128)(2,1)} reshape(bf16[32,20480]{1,0:T(8,128)(2,1)} %gather_fusion) | data formatting | bytes 2621440 | tf_op jit(solution)/shard_map/concatenate | solution.py:189
  52.1 5.9 %copy.115 = bf16[2,16,1,128,2,80]{3,5,1,0,4,2:T(8,128)(2,1)} copy(bf16[2,16,1,128,2,80]{5,4,3,1,0,2:T(2,128)(2,1)} %concatenate.44) | data formatting | bytes 2621440 | tf_op jit(solution)/shard_map/concatenate | solution.py:189
  59.0 3.3 %collective-permute-start.3 = (bf16[128,320]{0,1:T(8,128)(2,1)S(1)}, bf16[128,320]{0,1:T(8,128)(2,1)S(1)}, u32[]{:S(2)}, u32[]{:S(2)}) collective-permute-start(bf16[128,320]{0,1:T(8,128)(2,1)S(1)} %collective-permute-done.1), channel_id=1, source_target_pairs={{0,7},{1,0},{2,1},{3,2},{4,3},{5,4},{6,5},{7,6},{8,15},{9,8},{10,9... | collective-permute-start | bytes 245768 | tf_op jit(solution)/shard_map/ppermute | solution.py:31
  62.4 2.6 %collective-permute-done.2 = bf16[128,320]{0,1:T(8,128)(2,1)S(1)} collective-permute-done((bf16[128,320]{0,1:T(8,128)(2,1)S(1)}, bf16[128,320]{0,1:T(8,128)(2,1)S(1)}, u32[]{:S(2)}, u32[]{:S(2)}) %collective-permute-start.2) | collective-permute-done | bytes 81952 | tf_op jit(solution)/shard_map/ppermute | solution.py:26
  65.6 3.2 %collective-permute-start.5 = (bf16[128,320]{0,1:T(8,128)(2,1)S(1)}, bf16[128,320]{0,1:T(8,128)(2,1)}, u32[]{:S(2)}, u32[]{:S(2)}) collective-permute-start(bf16[128,320]{0,1:T(8,128)(2,1)S(1)} %collective-permute-done.3), channel_id=1, source_target_pairs={{0,7},{1,0},{2,1},{3,2},{4,3},{5,4},{6,5},{7,6},{8,15},{9,8},{10,9... | collective-permute-start | bytes 245768 | tf_op jit(solution)/shard_map/ppermute | solution.py:31
  68.8 1.8 %collective-permute-done.4 = bf16[128,320]{0,1:T(8,128)(2,1)S(1)} collective-permute-done((bf16[128,320]{0,1:T(8,128)(2,1)S(1)}, bf16[128,320]{0,1:T(8,128)(2,1)S(1)}, u32[]{:S(2)}, u32[]{:S(2)}) %collective-permute-start.4) | collective-permute-done | bytes 81952 | tf_op jit(solution)/shard_map/ppermute | solution.py:26
  72.3 1.1 dynamic_update_slice.26
  76.2 1.1 dynamic_update_slice.29
  78.3 1.1 dynamic_update_slice.30
  84.6 4.4 %reshape.500 = bf16[64,20480]{1,0:T(8,128)(2,1)} reshape(bf16[32,2,1,20480]{3,1,2,0:T(2,128)(2,1)} %all-to-all-done) | data formatting | bytes 5242880 | tf_op jit(solution)/shard_map/reshape | solution.py:186
  89.0 5.7 %gather_fusion.2 = bf16[32,20480]{1,0:T(8,128)(2,1)} fusion(bf16[64,20480]{1,0:T(8,128)(2,1)} %reshape.500, s32[1024]{0:T(1024)S(1)} %pad_clamp_fusion), kind=kCustom, calls=%fused_computation.2 | custom fusion | bytes 2621568 | tf_op jit(solution)/shard_map/gather | solution.py:186
  94.7 4.5 %concatenate.45 = bf16[2,16,1,128,2,80]{5,4,3,1,0,2:T(2,128)(2,1)} reshape(bf16[32,20480]{1,0:T(8,128)(2,1)} %gather_fusion.2) | data formatting | bytes 2621440 | tf_op jit(solution)/shard_map/concatenate | solution.py:189
  99.2 6.0 %copy.116 = bf16[2,16,1,128,2,80]{3,5,1,0,4,2:T(8,128)(2,1)} copy(bf16[2,16,1,128,2,80]{5,4,3,1,0,2:T(2,128)(2,1)} %concatenate.45) | data formatting | bytes 2621440 | tf_op jit(solution)/shard_map/concatenate | solution.py:189
  105.2 4.0 %fusion.3 = (f32[2,32,4,64]{3,2,1,0:T(4,128)S(1)}, f32[2,32,128,64,4]{2,3,4,1,0:T(8,128)S(1)}) fusion(pred[2,32,64,128]{3,2,1,0:T(8,128)(4,1)S(1)} %copy-done.1, bf16[2,64,4,40]{3,1,2,0:T(8,128)(2,1)S(1)} %copy.126, bf16[2,64,4,40]{3,1,2,0:T(8,128)(2,1)S(1)} %copy.125, bf16[2,16,1,128,2,80]{3,5,1,0,4,2:T(8,128)(2,1)} %copy.115, ...), kind=kOutput, calls=%fused_computation.11 | convolution fusion | flops 344604672 | bytes 11681792 | tf_op jit(solution)/shard_map/rtkgd,rjkpd->rjkgtp/dot_general | solution.py:64
  109.2 5.8 %convert_reduce_fusion = (f32[2,32,4,64]{3,2,1,0:T(4,128)S(1)}, f32[2,4,64]{2,1,0:T(4,128)S(1)}) fusion(f32[2,32,4,64]{3,2,1,0:T(4,128)S(1)} %get-tuple-element.18, f32[2,32,128,64,4]{2,3,4,1,0:T(8,128)S(1)} %get-tuple-element.19, pred[2,32,64,128]{3,2,1,0:T(8,128)(4,1)S(1)} %copy-done.1), kind=kLoop, calls=%fused_computation.9 | loop fusion | flops 16760320 | bytes 9046016 | tf_op jit(solution)/shard_map/reduce_sum | solution.py:72
  115.2 5.1 %multiply_reduce_fusion = f32[2,4,64,80]{3,2,1,0:T(8,128)S(1)} fusion(f32[2,32,4,64]{3,2,1,0:T(4,128)S(1)} %get-tuple-element.11, bf16[2,16,1,128,2,80]{3,5,1,0,4,2:T(8,128)(2,1)S(1)} %copy-done.3, bf16[2,16,1,128,2,80]{3,5,1,0,4,2:T(8,128)(2,1)S(1)} %copy-done.2, f32[2,32,128,64,4]{2,3,4,1,0:T(8,128)S(1)} %get-tuple-element.19, ...), kind=kOutput, calls=%fused_computation.10 | convolution fusion | flops 347168768 | bytes 11829248 | tf_op jit(solution)/shard_map/rjkgtp,rjkpd->rjkgtd/dot_general | solution.py:73
  120.9 3.4 %fusion.62 = f32[128,2560]{0,1:T(8,128)} fusion(bf16[128,320]{1,0:T(8,128)(2,1)S(1)} %convert_element_type.92, bf16[320,2560]{1,0:T(8,128)(2,1)} %param.12), kind=kOutput, calls=%fused_computation.112 | convolution fusion | flops 209715200 | bytes 3031040 | tf_op jit(solution)/shard_map/dot_general | solution.py:197
  124.4 38.4 %reduce-scatter.2.cloned.1.call-done = f32[128,320]{0,1:T(8,128)} async-done(((f32[128,2560]{0,1:T(8,128)}), f32[128,320]{0,1:T(8,128)}) %reduce-scatter.2.cloned.1.call-update) | async-done | bytes 163856 | tf_op jit(solution)/shard_map/reduce_scatter | solution.py:198
  (116 shorter events, 19.1 us)
Async XLA Ops:
  6.5 74.9 %copy-start = (bf16[2560,1,480]{0,2,1:T(8,128)(2,1)S(1)}, bf16[2560,1,480]{0,2,1:T(8,128)(2,1)}, u32[]{:S(2)}) copy-start(bf16[2560,1,480]{0,2,1:T(8,128)(2,1)} %param.11) | copy-start | bytes 7372804
  6.5 52.5 %collective-permute-start.1 = (bf16[128,320]{0,1:T(8,128)(2,1)}, bf16[128,320]{0,1:T(8,128)(2,1)S(1)}, u32[]{:S(2)}, u32[]{:S(2)}) collective-permute-start(bf16[128,320]{0,1:T(8,128)(2,1)} %param.9), channel_id=1, source_target_pairs={{0,7},{1,0},{2,1},{3,2},{4,3},{5,4},{6,5},{7,6},{8,15},{9,8},{10,9... | collective-permute-start | bytes 245768 | tf_op jit(solution)/shard_map/ppermute | solution.py:31
  12.4 46.5 %collective-permute-start = (bf16[128,320]{0,1:T(8,128)(2,1)}, bf16[128,320]{0,1:T(8,128)(2,1)S(1)}, u32[]{:S(2)}, u32[]{:S(2)}) collective-permute-start(bf16[128,320]{0,1:T(8,128)(2,1)} %param.9), channel_id=1, source_target_pairs={{0,1},{1,2},{2,3},{3,4},{4,5},{5,6},{6,7},{7,0},{8,9},{9,10},{10,1... | collective-permute-start | bytes 245768 | tf_op jit(solution)/shard_map/ppermute | solution.py:26
  29.3 8.1 %copy-start.7 = (s32[64,32]{0,1:T(8,128)S(1)}, s32[64,32]{0,1:T(8,128)}, u32[]{:S(2)}) copy-start(s32[64,32]{0,1:T(8,128)} %param.15) | copy-start | bytes 24580
  29.3 8.3 %copy-start.8 = (s32[64,32]{0,1:T(8,128)S(1)}, s32[64,32]{0,1:T(8,128)}, u32[]{:S(2)}) copy-start(s32[64,32]{0,1:T(8,128)} %param.14) | copy-start | bytes 24580
  29.3 8.4 %copy-start.11 = (s32[64]{0:T(128)S(1)}, s32[64]{0:T(128)}, u32[]{:S(2)}) copy-start(s32[64]{0:T(128)} %param.16) | copy-start | bytes 772
  29.3 10.3 %copy-start.4 = (bf16[128,320]{0,1:T(8,128)(2,1)S(1)}, bf16[128,320]{0,1:T(8,128)(2,1)}, u32[]{:S(2)}) copy-start(bf16[128,320]{0,1:T(8,128)(2,1)} %param.9) | copy-start | bytes 245764
  29.3 55.3 %all-to-all-start = ((bf16[32,2,1,20480]{3,1,2,0:T(2,128)(2,1)}), bf16[32,2,1,20480]{3,1,2,0:T(2,128)(2,1)}, u32[]{:S(2)}, u32[]{:S(2)}) async-start(bf16[32,2,1,20480]{3,1,2,0:T(2,128)(2,1)} %bitcast.129), calls=%async_computation | async-start | bytes 5242880 | tf_op jit(solution)/shard_map/all_to_all | solution.py:185
  37.1 125.7 %reduce-scatter.2.cloned.1.call-start = ((), (), s32[]{:S(2)}) async-start(), calls=%async_computation.2 | async-start | bytes 1474560 | tf_op jit(solution)/shard_map/reduce_scatter | solution.py:198
  58.9 6.1 %collective-permute-start.2 = (bf16[128,320]{0,1:T(8,128)(2,1)S(1)}, bf16[128,320]{0,1:T(8,128)(2,1)S(1)}, u32[]{:S(2)}, u32[]{:S(2)}) collective-permute-start(bf16[128,320]{0,1:T(8,128)(2,1)S(1)} %collective-permute-done), channel_id=1, source_target_pairs={{0,1},{1,2},{2,3},{3,4},{4,5},{5,6},{6,7},{7,0},{8,9},{9,10},{10,1... | collective-permute-start | bytes 245768 | tf_op jit(solution)/shard_map/ppermute | solution.py:26
  59.0 6.6 %collective-permute-start.3 = (bf16[128,320]{0,1:T(8,128)(2,1)S(1)}, bf16[128,320]{0,1:T(8,128)(2,1)S(1)}, u32[]{:S(2)}, u32[]{:S(2)}) collective-permute-start(bf16[128,320]{0,1:T(8,128)(2,1)S(1)} %collective-permute-done.1), channel_id=1, source_target_pairs={{0,7},{1,0},{2,1},{3,2},{4,3},{5,4},{6,5},{7,6},{8,15},{9,8},{10,9... | collective-permute-start | bytes 245768 | tf_op jit(solution)/shard_map/ppermute | solution.py:31
  65.0 5.7 %copy-start.5 = (bf16[128,320]{0,1:T(8,128)(2,1)}, bf16[128,320]{0,1:T(8,128)(2,1)S(1)}, u32[]{:S(2)}) copy-start(bf16[128,320]{0,1:T(8,128)(2,1)S(1)} %collective-permute-done.2) | copy-start | bytes 245764
  65.0 5.7 %collective-permute-start.4 = (bf16[128,320]{0,1:T(8,128)(2,1)S(1)}, bf16[128,320]{0,1:T(8,128)(2,1)S(1)}, u32[]{:S(2)}, u32[]{:S(2)}) collective-permute-start(bf16[128,320]{0,1:T(8,128)(2,1)S(1)} %collective-permute-done.2), channel_id=1, source_target_pairs={{0,1},{1,2},{2,3},{3,4},{4,5},{5,6},{6,7},{7,0},{8,9},{9,10},{10,1... | collective-permute-start | bytes 245768 | tf_op jit(solution)/shard_map/ppermute | solution.py:26
  65.6 11.7 %collective-permute-start.5 = (bf16[128,320]{0,1:T(8,128)(2,1)S(1)}, bf16[128,320]{0,1:T(8,128)(2,1)}, u32[]{:S(2)}, u32[]{:S(2)}) collective-permute-start(bf16[128,320]{0,1:T(8,128)(2,1)S(1)} %collective-permute-done.3), channel_id=1, source_target_pairs={{0,7},{1,0},{2,1},{3,2},{4,3},{5,4},{6,5},{7,6},{8,15},{9,8},{10,9... | collective-permute-start | bytes 245768 | tf_op jit(solution)/shard_map/ppermute | solution.py:31
  70.6 8.8 %collective-permute-start.6 = (bf16[128,320]{0,1:T(8,128)(2,1)S(1)}, bf16[128,320]{0,1:T(8,128)(2,1)}, u32[]{:S(2)}, u32[]{:S(2)}) collective-permute-start(bf16[128,320]{0,1:T(8,128)(2,1)S(1)} %collective-permute-done.4), channel_id=1, source_target_pairs={{0,1},{1,2},{2,3},{3,4},{4,5},{5,6},{6,7},{7,0},{8,9},{9,10},{10,1... | collective-permute-start | bytes 245768 | tf_op jit(solution)/shard_map/ppermute | solution.py:26
  71.3 10.1 %copy-start.10 = (f32[2560]{0:T(1024)S(1)}, f32[2560]{0:T(1024)}, u32[]{:S(2)}) copy-start(f32[2560]{0:T(1024)} %param.10) | copy-start | bytes 30724
  77.3 5.8 %copy-start.9 = (f32[40]{0:T(128)S(1)}, f32[40]{0:T(128)}, u32[]{:S(2)}) copy-start(f32[40]{0:T(128)} %negate_power_fusion) | copy-start | bytes 484
  99.2 6.0 %copy-start.1 = (pred[2,32,64,128]{3,2,1,0:T(8,128)(4,1)S(1)}, pred[2,32,64,128]{3,2,1,0:T(8,128)(4,1)}, u32[]{:S(2)}) copy-start(pred[2,32,64,128]{3,2,1,0:T(8,128)(4,1)} %fusion.9) | copy-start | bytes 1572868
  109.2 5.9 %copy-start.2 = (bf16[2,16,1,128,2,80]{3,5,1,0,4,2:T(8,128)(2,1)S(1)}, bf16[2,16,1,128,2,80]{3,5,1,0,4,2:T(8,128)(2,1)}, u32[]{:S(2)}) copy-start(bf16[2,16,1,128,2,80]{3,5,1,0,4,2:T(8,128)(2,1)} %copy.115) | copy-start | bytes 3932164
  109.2 5.9 %copy-start.3 = (bf16[2,16,1,128,2,80]{3,5,1,0,4,2:T(8,128)(2,1)S(1)}, bf16[2,16,1,128,2,80]{3,5,1,0,4,2:T(8,128)(2,1)}, u32[]{:S(2)}) copy-start(bf16[2,16,1,128,2,80]{3,5,1,0,4,2:T(8,128)(2,1)} %copy.116) | copy-start | bytes 3932164
  115.2 5.1 %copy-start.6 = (bf16[128,1,1,80]{3,0,2,1:T(8,128)(2,1)S(1)}, bf16[128,1,1,80]{3,0,2,1:T(8,128)(2,1)}, u32[]{:S(2)}) copy-start(bf16[128,1,1,80]{3,0,2,1:T(8,128)(2,1)} %copy.129) | copy-start | bytes 61444
Sparse Core Ops, SparseCore 0:
  124.5 38.2 reduce-scatter.1
